TPU v7x, 32 devices: a whole 2x2x4 slice. The times are simulated.
32 devices in a mesh: dp: 16 (over z, y, x), mp: 2 (over core).
Axes of the slice: x: 2, y: 2, z: 4, core: 2. Of those that a mesh axis runs over, the one named last changes fastest.
Arguments:
- hidden: bfloat16 [2048, 4096], P('dp', 'mp'), may hold values from -6 to 6
- attended: bfloat16 [2048, 4096], P('dp', 'mp'), may hold values from -6 to 6
- query_cotangent: bfloat16 [2048, 4096], P('dp', 'mp'), may hold values from -1.5 to 1.5
- output_cotangent: bfloat16 [2048, 4096], P('dp', 'mp'), may hold values from -1.5 to 1.5
- query_projection_weight: bfloat16 [4096, 4096], P('dp', 'mp'), may hold values from -0.09375 to 0.09375
- output_projection_weight: bfloat16 [4096, 4096], P('dp', 'mp'), may hold values from -0.09375 to 0.09375
- narrower: bfloat16 [256, 16, 4096], P('dp', None, 'mp'), may hold values from -0.09375 to 0.09375
- widener: bfloat16 [256, 16, 4096], P('dp', None, 'mp'), may hold values from -0.375 to 0.375
- reducer: bfloat16 [256, 16, 4096], P('dp', None, 'mp'), may hold values from -0.09375 to 0.09375
- enlarger: bfloat16 [256, 16, 4096], P('dp', None, 'mp'), may hold values from -0.375 to 0.375
- block_adapter: int32 [512], P('dp'), may hold values from 0 to 255, as said below
- block_fill: int32 [512], P('dp'), may hold values from 1 to 4
Outputs:
- queries: bfloat16 [2048, 4096], P('dp', 'mp')
- projected: bfloat16 [2048, 4096], P('dp', 'mp')
- hidden_state_gradient: bfloat16 [2048, 4096], P('dp', 'mp')
- attention_output_gradient: bfloat16 [2048, 4096], P('dp', 'mp')
- narrower_gradient: float32 [256, 16, 4096], P('dp', None, 'mp')
- widener_gradient: float32 [256, 16, 4096], P('dp', None, 'mp')
- reducer_gradient: float32 [256, 16, 4096], P('dp', None, 'mp')
- enlarger_gradient: float32 [256, 16, 4096], P('dp', None, 'mp')
Inputs may be any that keep to these rules, and one draw needn't show every extreme that they name: `block_adapter`: the owner of adapter e is e // 16. Among the 32 blocks of one group (one index of dp), at most 2 have adapters of one owner, and some owner has exactly 2 blocks in every group.
All inputs are finite; a program needn't handle non-finite values.
Results may differ from a plain program's by a relative error of at most 0.015.
Values may be sent and summed in bfloat16 or wider, within the bound.
A program may use at most 128 MiB of HBM per device.

v0:
```python
import jax
import jax.numpy as jnp
from jax import lax
from jax.sharding import Mesh, PartitionSpec as P

adapter_scale = 2.0


def product(left, right, contract):
    return lax.dot_general(
        left, right, ((contract[:1], contract[1:]), ((), ())), preferred_element_type=jnp.float32
    )


def one_hot(condition):
    return condition.astype(jnp.bfloat16)


def iota(shape, dimension):
    return lax.broadcasted_iota(jnp.int32, shape, dimension)


def stacked_columns(values, parts):
    wide = values.shape[1] // parts
    return jnp.concatenate([values[:, i * wide : (i + 1) * wide] for i in range(parts)], axis=0)


def unstacked_columns(values, parts):
    rows = values.shape[0] // parts
    return jnp.concatenate([values[i * rows : (i + 1) * rows] for i in range(parts)], axis=1)


def exchange(values, axis):
    return lax.all_to_all(values, axis, split_axis=0, concat_axis=0, tiled=True)


def on_device(
    hidden,
    attended,
    query_cotangent,
    output_cotangent,
    query_projection_weight,
    output_projection_weight,
    narrower,
    widener,
    reducer,
    enlarger,
    block_adapter,
    block_fill,
):
    dp = ("far", "near")
    far = lax.axis_size("far")
    owners = far * lax.axis_size("near")
    tokens = hidden.shape[0]
    group_blocks = block_adapter.shape[0]
    width = tokens // group_blocks
    capacity = -(-group_blocks // owners)
    per_owner, rank = narrower.shape[:2]
    lanes = -(-per_owner // 128) * 128
    query_rows = lax.all_gather(query_projection_weight, "near", axis=0, tiled=True)
    output_rows = lax.all_gather(output_projection_weight, "near", axis=0, tiled=True)
    row_ids = iota((group_blocks, width), 1)
    live = one_hot(row_ids < block_fill[:, None]).reshape(tokens, 1)
    query_masked = query_cotangent * live
    output_masked = output_cotangent * live
    owner_of = block_adapter // per_owner
    later_ids = iota((group_blocks, group_blocks), 0)
    earlier_ids = iota((group_blocks, group_blocks), 1)
    before = (owner_of[:, None] == owner_of[None, :]) & (earlier_ids < later_ids)
    position = jnp.sum(before.astype(jnp.int32), axis=1)
    slot_of = owner_of * capacity + position
    row_of = (slot_of[:, None] * width + row_ids).reshape(1, tokens)
    table = one_hot(iota((owners * capacity * width, tokens), 0) == row_of)
    local_of = jnp.broadcast_to((block_adapter % per_owner)[:, None], (group_blocks, width))
    local_hot = one_hot(iota((tokens, lanes), 1) == local_of.reshape(tokens, 1))
    sent = jnp.concatenate(
        [
            product(table, part, (1, 0)).astype(jnp.bfloat16)
            for part in (local_hot, hidden, attended, query_masked, output_masked)
        ],
        axis=1,
    )
    received = exchange(sent, dp)
    model, query = (hidden.shape[1], attended.shape[1])
    ends = [lanes, lanes + model, lanes + model + query, lanes + model + 2 * query]
    hot, hid, att, qcot, ocot = jnp.split(received, ends, axis=1)
    many = per_owner * rank
    spread = one_hot(iota((lanes, many), 0) == iota((lanes, many), 1) // rank)
    own = product(hot, spread, (1, 0))
    fold = one_hot(iota((many, rank), 0) % rank == iota((many, rank), 1))
    factors = [f.reshape(many, f.shape[2]) for f in (narrower, reducer, widener, enlarger)]
    folded = jnp.concatenate(
        [
            product((product(x, f, (1, 1)) * own).astype(jnp.bfloat16), fold, (1, 0))
            for x, f in zip((hid, att, qcot, ocot), factors)
        ],
        axis=1,
    ).astype(jnp.bfloat16)
    ranks = lax.psum(folded, "mp")
    query_rank, output_rank, query_back, output_back = [
        (product(ranks[:, i * rank : (i + 1) * rank], fold, (1, 1)) * own).astype(jnp.bfloat16)
        for i in range(4)
    ]
    down_query, down_output, up_query, up_output = factors
    returned = exchange(
        jnp.concatenate(
            [
                (adapter_scale * product(r, f, (1, 0))).astype(jnp.bfloat16)
                for r, f in (
                    (query_rank, up_query),
                    (output_rank, up_output),
                    (query_back, down_query),
                    (output_back, down_output),
                )
            ],
            axis=1,
        ),
        dp,
    )

    def gradient(ranks, rows, like):
        return (adapter_scale * product(ranks, rows, (0, 0))).reshape(like.shape)

    narrower_gradient = gradient(query_back, hid, narrower)
    widener_gradient = gradient(query_rank, qcot, widener)
    reducer_gradient = gradient(output_back, att, reducer)
    enlarger_gradient = gradient(output_rank, ocot, enlarger)
    hid_full = lax.all_gather(hidden, "mp", axis=1, tiled=True)
    att_full = lax.all_gather(attended, "mp", axis=1, tiled=True)
    depth = hid_full.shape[1] // far
    inputs = exchange(
        jnp.concatenate([stacked_columns(hid_full, far), stacked_columns(att_full, far)], axis=1),
        "far",
    )
    cotangents = [
        lax.all_gather(masked, "far", axis=0, tiled=True)
        for masked in (query_masked, output_masked)
    ]

    def forward(values, weight):
        part = product(values, weight, (1, 0)).astype(jnp.bfloat16)
        parts = exchange(part, "far").reshape(far, tokens, weight.shape[1])
        return jnp.sum(parts.astype(jnp.float32), axis=0)

    def backward(masked, weight):
        part = product(masked, weight, (1, 1)).astype(jnp.bfloat16)
        whole = unstacked_columns(exchange(part, "far"), far)
        return lax.psum_scatter(whole, "mp", scatter_dimension=1, tiled=True)

    base = [
        forward(inputs[:, :depth], query_rows),
        forward(inputs[:, depth:], output_rows),
        backward(cotangents[0], query_rows).astype(jnp.float32),
        backward(cotangents[1], output_rows).astype(jnp.float32),
    ]
    starts = [query, query + model, query + 2 * model]
    adapter_terms = [product(table, part, (0, 0)) for part in jnp.split(returned, starts, axis=1)]
    queries, projected, hidden_state_gradient, attention_output_gradient = [
        (b + t).astype(jnp.bfloat16) for b, t in zip(base, adapter_terms)
    ]
    return (
        queries,
        projected,
        hidden_state_gradient,
        attention_output_gradient,
        narrower_gradient,
        widener_gradient,
        reducer_gradient,
        enlarger_gradient,
    )


def solution(mesh):
    count = mesh.shape["dp"]
    far = 1
    while far * far < count or count % far:
        far += 1
    split = Mesh(mesh.devices.reshape(far, count // far, mesh.shape["mp"]), ("far", "near", "mp"))
    dp = ("far", "near")
    rows, factors = (P(dp, "mp"), P(dp, None, "mp"))
    return jax.shard_map(
        on_device,
        mesh=split,
        in_specs=(rows,) * 6 + (factors,) * 4 + (P(dp),) * 2,
        out_specs=(rows,) * 4 + (factors,) * 4,
        check_vma=False,
    )
```

profile of v0, /device:TPU:12, one launch (start us, length us, event | category | flops | bytes accessed | tf_op | source)
XLA Modules:
  0.0 492.3 jit_solution(7176359094371279426)
XLA Ops:
  9.6 2.4 broadcast_multiply_fusion
  16.8 7.2 %all-to-all-start.2 = ((bf16[16,8,8320]{2,1,0:T(8,128)(2,1)}), bf16[16,8,8320]{2,1,0:T(8,128)(2,1)S(1)}, u32[]{:S(2)}, u32[]{:S(2)}) async-start(bf16[16,8,8320]{2,1,0:T(8,128)(2,1)} %bitcast.73), calls=%async_computation.2 | async-start | bytes 4259840 | tf_op jit(solution)/shard_map/all_to_all | solution.py:34
  24.5 2.1 fusion.93
  26.6 5.1 %all-gather.9.cloned.1.call-done = bf16[128,4096]{1,0:T(8,128)(2,1)} async-done(((bf16[128,2048]{1,0:T(8,128)(2,1)}), bf16[128,4096]{1,0:T(8,128)(2,1)}) %all-gather.9.cloned.1.call-update) | async-done | bytes 1048592 | tf_op jit(solution)/shard_map/all_gather | solution.py:129
  33.2 13.9 %maximum_maximum_fusion = bf16[512,2048]{1,0:T(8,128)(2,1)} fusion(bf16[128,1024]{1,0:T(8,128)(2,1)S(1)} %get-tuple-element.21, bf16[128,1024]{1,0:T(8,128)(2,1)S(1)} %get-tuple-element.22, bf16[128,1024]{1,0:T(8,128)(2,1)S(1)} %get-tuple-element.23, bf16[128,1024]{1,0:T(8,128)(2,1)S(1)} %get-tuple-element.20, bf16[128,1024]{1,0:T(8,128)(2,1)S(1)} %copy-done.9, ...), kind=kLoop, calls=%fused_computation.32 | loop fusion | flops 16777216 | bytes 4194304 | tf_op jit(solution)/shard_map/concatenate | solution.py:132
  47.1 59.3 %all-to-all-done.2 = bf16[16,8,8320]{2,1,0:T(8,128)(2,1)S(1)} async-done(((bf16[16,8,8320]{2,1,0:T(8,128)(2,1)}), bf16[16,8,8320]{2,1,0:T(8,128)(2,1)S(1)}, u32[]{:S(2)}, u32[]{:S(2)}) %all-to-all-start.2) | async-done | bytes 2129952 | tf_op jit(solution)/shard_map/all_to_all | solution.py:34
  106.4 4.5 all-to-all-start
  110.9 48.8 %all-gather.11.cloned.1.call-done = bf16[1024,2048]{1,0:T(8,128)(2,1)} async-done(((bf16[256,2048]{1,0:T(8,128)(2,1)}), bf16[1024,2048]{1,0:T(8,128)(2,1)}) %all-gather.11.cloned.1.call-update) | async-done | bytes 4194320 | tf_op jit(solution)/shard_map/all_gather | solution.py:60
  159.7 6.2 %convolution_convert_fusion.7 = bf16[512,1024]{1,0:T(8,128)(2,1)} fusion(bf16[512,2048]{1,0:T(8,128)(2,1)} %all-gather.15.cloned.1.call-done, bf16[1024,2048]{1,0:T(8,128)(2,1)} %all-gather.11.cloned.1.call-done), kind=kOutput, calls=%fused_computation.35 | convolution fusion | flops 2148007936 | bytes 7340032 | tf_op jit(solution)/shard_map/dot_general | solution.py:10
  165.9 5.1 %all-to-all-start.5 = ((bf16[4,128,1024]{2,1,0:T(8,128)(2,1)}), bf16[4,128,1024]{2,1,0:T(8,128)(2,1)}, u32[]{:S(2)}, u32[]{:S(2)}) async-start(bf16[4,128,1024]{2,1,0:T(8,128)(2,1)} %bitcast.86), calls=%async_computation.5 | async-start | bytes 2097152 | tf_op jit(solution)/shard_map/all_to_all | solution.py:34
  171.0 56.3 %all-gather.17.cloned.1.call-done = bf16[512,2048]{1,0:T(8,128)(2,1)} async-done(((bf16[128,2048]{1,0:T(8,128)(2,1)}), bf16[512,2048]{1,0:T(8,128)(2,1)}) %all-gather.17.cloned.1.call-update) | async-done | bytes 2097168 | tf_op jit(solution)/shard_map/all_gather | solution.py:136
  227.3 55.3 %all-gather.13.cloned.1.call-done = bf16[1024,2048]{1,0:T(8,128)(2,1)} async-done(((bf16[256,2048]{1,0:T(8,128)(2,1)}), bf16[1024,2048]{1,0:T(8,128)(2,1)}) %all-gather.13.cloned.1.call-update) | async-done | bytes 4194320 | tf_op jit(solution)/shard_map/all_gather | solution.py:61
  282.6 6.2 %convolution_convert_fusion.6 = bf16[512,1024]{1,0:T(8,128)(2,1)} fusion(bf16[512,2048]{1,0:T(8,128)(2,1)} %all-gather.17.cloned.1.call-done, bf16[1024,2048]{1,0:T(8,128)(2,1)} %all-gather.13.cloned.1.call-done), kind=kOutput, calls=%fused_computation.34 | convolution fusion | flops 2148007936 | bytes 7340032 | tf_op jit(solution)/shard_map/dot_general | solution.py:10
  288.8 5.1 %all-to-all-start.6 = ((bf16[4,128,1024]{2,1,0:T(8,128)(2,1)}), bf16[4,128,1024]{2,1,0:T(8,128)(2,1)}, u32[]{:S(2)}, u32[]{:S(2)}) async-start(bf16[4,128,1024]{2,1,0:T(8,128)(2,1)} %bitcast.87), calls=%async_computation.7 | async-start | bytes 2097152 | tf_op jit(solution)/shard_map/all_to_all | solution.py:34
  293.9 6.2 %convolution_convert_fusion = bf16[512,2048]{1,0:T(8,128)(2,1)} fusion(bf16[1024,2048]{1,0:T(8,128)(2,1)} %all-gather.13.cloned.1.call-done, bf16[512,2048]{1,0:T(8,128)(2,1)} %bitcast.1), kind=kOutput, calls=%fused_computation.2 | convolution fusion | flops 2148532224 | bytes 7340032 | tf_op jit(solution)/shard_map/dot_general | solution.py:10
  300.1 16.1 %all-to-all-done.6 = bf16[4,128,1024]{2,1,0:T(8,128)(2,1)} async-done(((bf16[4,128,1024]{2,1,0:T(8,128)(2,1)}), bf16[4,128,1024]{2,1,0:T(8,128)(2,1)}, u32[]{:S(2)}, u32[]{:S(2)}) %all-to-all-start.6) | async-done | bytes 1048608 | tf_op jit(solution)/shard_map/all_to_all | solution.py:34
  316.2 7.8 %all-to-all-start.4 = ((bf16[4,128,2048]{2,1,0:T(8,128)(2,1)}), bf16[4,128,2048]{2,1,0:T(8,128)(2,1)}, u32[]{:S(2)}, u32[]{:S(2)}) async-start(bf16[4,128,2048]{2,1,0:T(8,128)(2,1)} %bitcast.79), calls=%async_computation.4 | async-start | bytes 4194304 | tf_op jit(solution)/shard_map/all_to_all | solution.py:34
  324.1 1.8 fusion.27
  326.6 1.8 fusion.25
  328.4 6.2 %convolution_convert_fusion.1 = bf16[512,2048]{1,0:T(8,128)(2,1)} fusion(bf16[1024,2048]{1,0:T(8,128)(2,1)} %all-gather.11.cloned.1.call-done, bf16[512,2048]{1,0:T(8,128)(2,1)} %bitcast.1), kind=kOutput, calls=%fused_computation.3 | convolution fusion | flops 2148532224 | bytes 7340032 | tf_op jit(solution)/shard_map/dot_general | solution.py:10
  334.6 33.9 %all-to-all-done.4 = bf16[4,128,2048]{2,1,0:T(8,128)(2,1)} async-done(((bf16[4,128,2048]{2,1,0:T(8,128)(2,1)}), bf16[4,128,2048]{2,1,0:T(8,128)(2,1)}, u32[]{:S(2)}, u32[]{:S(2)}) %all-to-all-start.4) | async-done | bytes 2097184 | tf_op jit(solution)/shard_map/all_to_all | solution.py:34
  368.4 7.8 %all-to-all-start.1 = ((bf16[4,128,2048]{2,1,0:T(8,128)(2,1)}), bf16[4,128,2048]{2,1,0:T(8,128)(2,1)}, u32[]{:S(2)}, u32[]{:S(2)}) async-start(bf16[4,128,2048]{2,1,0:T(8,128)(2,1)} %bitcast.78), calls=%async_computation.1 | async-start | bytes 4194304 | tf_op jit(solution)/shard_map/all_to_all | solution.py:34
  378.1 3.4 psum.7
  385.9 34.8 %all-to-all-done.1 = bf16[4,128,2048]{2,1,0:T(8,128)(2,1)} async-done(((bf16[4,128,2048]{2,1,0:T(8,128)(2,1)}), bf16[4,128,2048]{2,1,0:T(8,128)(2,1)}, u32[]{:S(2)}, u32[]{:S(2)}) %all-to-all-start.1) | async-done | bytes 2097184 | tf_op jit(solution)/shard_map/all_to_all | solution.py:34
  420.7 7.6 %all-to-all-start.3 = ((bf16[16,8,8192]{2,1,0:T(8,128)(2,1)}), bf16[16,8,8192]{2,1,0:T(8,128)(2,1)}, u32[]{:S(2)}, u32[]{:S(2)}) async-start(bf16[16,8,8192]{2,1,0:T(8,128)(2,1)} %maximum_bitcast_fusion), calls=%async_computation.3 | async-start | bytes 4194304 | tf_op jit(solution)/shard_map/all_to_all | solution.py:34
  440.5 2.1 convert_reduce_fusion
  442.6 2.1 convert_reduce_fusion.1
  444.6 31.7 %all-to-all-done.3 = bf16[16,8,8192]{2,1,0:T(8,128)(2,1)} async-done(((bf16[16,8,8192]{2,1,0:T(8,128)(2,1)}), bf16[16,8,8192]{2,1,0:T(8,128)(2,1)}, u32[]{:S(2)}, u32[]{:S(2)}) %all-to-all-start.3) | async-done | bytes 2097184 | tf_op jit(solution)/shard_map/all_to_all | solution.py:34
  476.4 2.2 fusion.5
  478.5 2.2 fusion.4
  480.7 2.3 fusion.7
  483.1 2.3 fusion.6
  (94 shorter events, 28.1 us)
Async XLA Ops:
  7.2 318.8 %copy-start = (bf16[16,16,2048]{2,1,0:T(8,128)(2,1)S(1)}, bf16[16,16,2048]{2,1,0:T(8,128)(2,1)}, u32[]{:S(2)}) copy-start(bf16[16,16,2048]{2,1,0:T(8,128)(2,1)} %param.19) | copy-start | bytes 3145732
  7.2 17.3 %all-gather.7.cloned.1.call-start = ((), (), s32[]{:S(2)}) async-start(), calls=%async_computation.9 | async-start | bytes 1572864 | tf_op jit(solution)/shard_map/all_gather | solution.py:128
  7.9 23.8 %all-gather.9.cloned.1.call-start = ((), (), s32[]{:S(2)}) async-start(), calls=%async_computation.10 | async-start | bytes 1572864 | tf_op jit(solution)/shard_map/all_gather | solution.py:129
  8.7 4.5 copy-start.14
  8.7 102.2 %all-gather.15.cloned.1.call-start = ((), (), s32[]{:S(2)}) async-start(), calls=%async_computation.13 | async-start | bytes 2621440 | tf_op jit(solution)/shard_map/all_gather | solution.py:136
  9.6 4.6 copy-start.4
  11.9 2.5 copy-start.5
  11.9 2.8 copy-start.2
  12.0 147.7 %all-gather.11.cloned.1.call-start = ((), (), s32[]{:S(2)}) async-start(), calls=%async_computation.11 | async-start | bytes 5242880 | tf_op jit(solution)/shard_map/all_gather | solution.py:60
  12.5 2.5 copy-start.1
  12.6 214.8 %all-gather.17.cloned.1.call-start = ((), (), s32[]{:S(2)}) async-start(), calls=%async_computation.15 | async-start | bytes 2621440 | tf_op jit(solution)/shard_map/all_gather | solution.py:136
  15.4 1.4 copy-start.3
  16.8 89.7 %all-to-all-start.2 = ((bf16[16,8,8320]{2,1,0:T(8,128)(2,1)}), bf16[16,8,8320]{2,1,0:T(8,128)(2,1)S(1)}, u32[]{:S(2)}, u32[]{:S(2)}) async-start(bf16[16,8,8320]{2,1,0:T(8,128)(2,1)} %bitcast.73), calls=%async_computation.2 | async-start | bytes 4259840 | tf_op jit(solution)/shard_map/all_to_all | solution.py:34
  23.9 258.7 %all-gather.13.cloned.1.call-start = ((), (), s32[]{:S(2)}) async-start(), calls=%async_computation.12 | async-start | bytes 5242880 | tf_op jit(solution)/shard_map/all_gather | solution.py:61
  31.8 1.3 copy-start.9
  31.8 1.4 copy-start.10
  31.8 1.4 copy-start.11
  106.4 59.4 %all-to-all-start = ((bf16[4,128,2048]{2,1,0:T(8,128)(2,1)}), bf16[4,128,2048]{2,1,0:T(8,128)(2,1)}, u32[]{:S(2)}, u32[]{:S(2)}) async-start(bf16[4,128,2048]{2,1,0:T(8,128)(2,1)} %bitcast.72), calls=%async_computation | async-start | bytes 4194304 | tf_op jit(solution)/shard_map/all_to_all | solution.py:34
  165.9 122.9 %all-to-all-start.5 = ((bf16[4,128,1024]{2,1,0:T(8,128)(2,1)}), bf16[4,128,1024]{2,1,0:T(8,128)(2,1)}, u32[]{:S(2)}, u32[]{:S(2)}) async-start(bf16[4,128,1024]{2,1,0:T(8,128)(2,1)} %bitcast.86), calls=%async_computation.5 | async-start | bytes 2097152 | tf_op jit(solution)/shard_map/all_to_all | solution.py:34
  288.8 27.4 %all-to-all-start.6 = ((bf16[4,128,1024]{2,1,0:T(8,128)(2,1)}), bf16[4,128,1024]{2,1,0:T(8,128)(2,1)}, u32[]{:S(2)}, u32[]{:S(2)}) async-start(bf16[4,128,1024]{2,1,0:T(8,128)(2,1)} %bitcast.87), calls=%async_computation.7 | async-start | bytes 2097152 | tf_op jit(solution)/shard_map/all_to_all | solution.py:34
  316.2 52.3 %all-to-all-start.4 = ((bf16[4,128,2048]{2,1,0:T(8,128)(2,1)}), bf16[4,128,2048]{2,1,0:T(8,128)(2,1)}, u32[]{:S(2)}, u32[]{:S(2)}) async-start(bf16[4,128,2048]{2,1,0:T(8,128)(2,1)} %bitcast.79), calls=%async_computation.4 | async-start | bytes 4194304 | tf_op jit(solution)/shard_map/all_to_all | solution.py:34
  368.4 52.3 %all-to-all-start.1 = ((bf16[4,128,2048]{2,1,0:T(8,128)(2,1)}), bf16[4,128,2048]{2,1,0:T(8,128)(2,1)}, u32[]{:S(2)}, u32[]{:S(2)}) async-start(bf16[4,128,2048]{2,1,0:T(8,128)(2,1)} %bitcast.78), calls=%async_computation.1 | async-start | bytes 4194304 | tf_op jit(solution)/shard_map/all_to_all | solution.py:34
  381.4 1.6 copy-start.6
  381.4 2.0 copy-start.7
  381.8 2.0 copy-start.12
  382.7 1.3 copy-start.8
  420.7 55.6 %all-to-all-start.3 = ((bf16[16,8,8192]{2,1,0:T(8,128)(2,1)}), bf16[16,8,8192]{2,1,0:T(8,128)(2,1)}, u32[]{:S(2)}, u32[]{:S(2)}) async-start(bf16[16,8,8192]{2,1,0:T(8,128)(2,1)} %maximum_bitcast_fusion), calls=%async_computation.3 | async-start | bytes 4194304 | tf_op jit(solution)/shard_map/all_to_all | solution.py:34
  428.3 2.7 copy-start.13
  428.3 52.4 %reduce-scatter.5.cloned.1.call-start = ((), (), s32[]{:S(2)}) async-start(), calls=%async_computation.16 | async-start | bytes 1572864 | tf_op jit(solution)/shard_map/reduce_scatter | solution.py:148
  430.7 52.4 %reduce-scatter.3.cloned.1.call-start = ((), (), s32[]{:S(2)}) async-start(), calls=%async_computation.14 | async-start | bytes 1572864 | tf_op jit(solution)/shard_map/reduce_scatter | solution.py:148
Sparse Core Ops, SparseCore 0:
  9.5 10.3 all-gather.6
  21.5 10.1 all-gather.8
  33.9 69.3 all-gather.14
  105.0 54.6 all-gather.10
  161.7 65.5 all-gather.16
  229.0 53.5 all-gather.12
  431.4 9.5 reduce-scatter.4
  443.2 9.5 reduce-scatter.2
where the time goes:
time: 493 us; the launch traced here: 492 us
  waiting for transfers between devices  344 us (70%)
  matrix products  51 us (10%)
  starting transfers between devices  45.6 us (9%)
  other arithmetic  25.2 us (5%)
  between operations  14.5 us (3%)
  local copies, waits for them, and re-layouts  8.27 us (2%)
    all_to_all x7, waiting for transfers between devices, exchange(): return lax.all_to_all(values, axis, split_axis=0, concat_axis=0, tiled=True)  176 us
    all_gather x2, waiting for transfers between devices, on_device(): lax.all_gather(masked, 'far', axis=0, tiled=True)  56.3 us
    all_gather x1, waiting for transfers between devices, on_device(): lax.all_gather(output_projection_weight, 'near', axis=0, tiled=True)  55.3 us
    dot_general x30, matrix products, product(): lax.dot_general(left, right, ((contract[:1], contract[1:]), ((), ())), pr...  51 us
    all_gather x1, waiting for transfers between devices, on_device(): lax.all_gather(query_projection_weight, 'near', axis=0, tiled=True)  48.8 us
    all_to_all x7, starting transfers between devices, exchange(): return lax.all_to_all(values, axis, split_axis=0, concat_axis=0, tiled=True)  45 us
    concatenate x1, other arithmetic, on_device(): jnp.concatenate([stacked_columns(hid_full, far), stacked_columns(att_full...  13.9 us
  transfers between devices with their start and end apart: 15, of which 9 were waited for; matrix products, arithmetic and copies ran while one was open for 16% of the time, Pallas kernels for 0%

commit v1 on v0

--- a/solution.py
+++ b/solution.py
@@ -57,8 +57,16 @@
     capacity = -(-group_blocks // owners)
     per_owner, rank = narrower.shape[:2]
     lanes = -(-per_owner // 128) * 128
-    query_rows = lax.all_gather(query_projection_weight, "near", axis=0, tiled=True)
-    output_rows = lax.all_gather(output_projection_weight, "near", axis=0, tiled=True)
+    query_rows, output_rows = jnp.split(
+        lax.all_gather(
+            jnp.concatenate([query_projection_weight, output_projection_weight], axis=1),
+            "near",
+            axis=0,
+            tiled=True,
+        ),
+        [query_projection_weight.shape[1]],
+        axis=1,
+    )
     row_ids = iota((group_blocks, width), 1)
     live = one_hot(row_ids < block_fill[:, None]).reshape(tokens, 1)
     query_masked = query_cotangent * live

time: 493 us -> 478 us (0.970)
  waiting for transfers between devices: 344 us -> 323 us
    all_gather x2 -> x1, waiting for transfers between devices: 104 us -> 83.1 us  [on_device(): lax.all_gather(jnp.concatenate([query_projection_weight, output_projectio...]
    all_gather x1, waiting for transfers between devices: 5.13 us -> 0.01 us  [on_device(): att_full = lax.all_gather(attended, 'mp', axis=1, tiled=True)]
  transfers between devices with their start and end apart: 15 -> 14, of which waited for: 9 -> 8; matrix products, arithmetic and copies ran while one was open for 16% -> 18% of each run, Pallas kernels for 0% -> 0%
where the time goes in v1:
time: 478 us; the launch traced here: 477 us
  waiting for transfers between devices  323 us (68%)
  matrix products  51.8 us (11%)
  starting transfers between devices  47.7 us (10%)
  other arithmetic  27.9 us (6%)
  between operations  14.5 us (3%)
  local copies, waits for them, and re-layouts  8.29 us (2%)
    all_to_all x7, waiting for transfers between devices, exchange(): return lax.all_to_all(values, axis, split_axis=0, concat_axis=0, tiled=True)  179 us
    all_gather x1, waiting for transfers between devices, on_device(): lax.all_gather(jnp.concatenate([query_projection_weight, output_projectio...  83.1 us
    all_gather x2, waiting for transfers between devices, on_device(): lax.all_gather(masked, 'far', axis=0, tiled=True)  56.3 us
    dot_general x30, matrix products, product(): lax.dot_general(left, right, ((contract[:1], contract[1:]), ((), ())), pr...  51.8 us
    all_to_all x7, starting transfers between devices, exchange(): return lax.all_to_all(values, axis, split_axis=0, concat_axis=0, tiled=True)  47.2 us
    concatenate x1, other arithmetic, on_device(): jnp.concatenate([stacked_columns(hid_full, far), stacked_columns(att_full...  13.9 us
  transfers between devices with their start and end apart: 14, of which 8 were waited for; matrix products, arithmetic and copies ran while one was open for 18% of the time, Pallas kernels for 0%

profile of v1, /device:TPU:12, one launch (start us, length us, event | category | flops | bytes accessed | tf_op | source)
XLA Modules:
  0.0 476.8 jit_solution(15776530752277415124)
XLA Ops:
  9.6 2.1 broadcast_multiply_fusion
  11.8 2.9 pad_maximum_fusion
  19.1 7.2 %all-to-all-start.2 = ((bf16[16,8,8320]{2,1,0:T(8,128)(2,1)}), bf16[16,8,8320]{2,1,0:T(8,128)(2,1)S(1)}, u32[]{:S(2)}, u32[]{:S(2)}) async-start(bf16[16,8,8320]{2,1,0:T(8,128)(2,1)} %bitcast.69), calls=%async_computation.2 | async-start | bytes 4259840 | tf_op jit(solution)/shard_map/all_to_all | solution.py:34
  26.3 2.1 fusion.114
  28.4 3.4 all-gather.6.cloned.1.call-done
  33.2 13.9 %maximum_maximum_fusion = bf16[512,2048]{1,0:T(8,128)(2,1)} fusion(bf16[128,1024]{1,0:T(8,128)(2,1)S(1)} %copy-done.10, bf16[128,1024]{1,0:T(8,128)(2,1)S(1)} %copy-done.11, bf16[128,1024]{1,0:T(8,128)(2,1)S(1)} %copy-done.12, bf16[128,1024]{1,0:T(8,128)(2,1)S(1)} %get-tuple-element.20, bf16[128,1024]{1,0:T(8,128)(2,1)S(1)} %get-tuple-element.17, ...), kind=kLoop, calls=%fused_computation.40 | loop fusion | flops 16777216 | bytes 4194304 | tf_op jit(solution)/shard_map/concatenate | solution.py:140
  47.1 61.7 %all-to-all-done.2 = bf16[16,8,8320]{2,1,0:T(8,128)(2,1)S(1)} async-done(((bf16[16,8,8320]{2,1,0:T(8,128)(2,1)}), bf16[16,8,8320]{2,1,0:T(8,128)(2,1)S(1)}, u32[]{:S(2)}, u32[]{:S(2)}) %all-to-all-start.2) | async-done | bytes 2129952 | tf_op jit(solution)/shard_map/all_to_all | solution.py:34
  108.8 4.5 all-to-all-start
  113.9 83.1 %all-gather.10.cloned.1.call-done = bf16[1024,4096]{1,0:T(8,128)(2,1)} async-done(((bf16[256,4096]{1,0:T(8,128)(2,1)}), bf16[1024,4096]{1,0:T(8,128)(2,1)}) %all-gather.10.cloned.1.call-update) | async-done | bytes 8388624 | tf_op jit(solution)/shard_map/all_gather | solution.py:61
  196.9 6.2 %fusion.26 = bf16[512,1024]{1,0:T(8,128)(2,1)} fusion(bf16[512,2048]{1,0:T(8,128)(2,1)} %all-gather.12.cloned.1.call-done, bf16[1024,4096]{1,0:T(8,128)(2,1)} %all-gather.10.cloned.1.call-done), kind=kOutput, calls=%fused_computation.43 | convolution fusion | flops 2148007936 | bytes 7340032 | tf_op jit(solution)/shard_map/dot_general | solution.py:10
  203.1 5.1 %all-to-all-start.5 = ((bf16[4,128,1024]{2,1,0:T(8,128)(2,1)}), bf16[4,128,1024]{2,1,0:T(8,128)(2,1)}, u32[]{:S(2)}, u32[]{:S(2)}) async-start(bf16[4,128,1024]{2,1,0:T(8,128)(2,1)} %bitcast.82), calls=%async_computation.5 | async-start | bytes 2097152 | tf_op jit(solution)/shard_map/all_to_all | solution.py:34
  208.2 56.3 %all-gather.14.cloned.1.call-done = bf16[512,2048]{1,0:T(8,128)(2,1)} async-done(((bf16[128,2048]{1,0:T(8,128)(2,1)}), bf16[512,2048]{1,0:T(8,128)(2,1)}) %all-gather.14.cloned.1.call-update) | async-done | bytes 2097168 | tf_op jit(solution)/shard_map/all_gather | solution.py:144
  264.5 6.2 %fusion.29 = bf16[512,1024]{1,0:T(8,128)(2,1)} fusion(bf16[512,2048]{1,0:T(8,128)(2,1)} %all-gather.14.cloned.1.call-done, bf16[1024,4096]{1,0:T(8,128)(2,1)} %all-gather.10.cloned.1.call-done), kind=kOutput, calls=%fused_computation.44 | convolution fusion | flops 2148007936 | bytes 7340032 | tf_op jit(solution)/shard_map/dot_general | solution.py:10
  270.7 7.3 %all-to-all-start.6 = ((bf16[4,128,1024]{2,1,0:T(8,128)(2,1)}), bf16[4,128,1024]{2,1,0:T(8,128)(2,1)}, u32[]{:S(2)}, u32[]{:S(2)}) async-start(bf16[4,128,1024]{2,1,0:T(8,128)(2,1)} %bitcast.83), calls=%async_computation.7 | async-start | bytes 2097152 | tf_op jit(solution)/shard_map/all_to_all | solution.py:34
  278.0 6.2 %fusion.8 = bf16[512,2048]{1,0:T(8,128)(2,1)} fusion(bf16[1024,4096]{1,0:T(8,128)(2,1)} %all-gather.10.cloned.1.call-done, bf16[512,2048]{1,0:T(8,128)(2,1)} %bitcast.1), kind=kOutput, calls=%fused_computation.10 | convolution fusion | flops 2148532224 | bytes 7340032 | tf_op jit(solution)/shard_map/dot_general | solution.py:10
  284.2 16.6 %all-to-all-done.6 = bf16[4,128,1024]{2,1,0:T(8,128)(2,1)} async-done(((bf16[4,128,1024]{2,1,0:T(8,128)(2,1)}), bf16[4,128,1024]{2,1,0:T(8,128)(2,1)}, u32[]{:S(2)}, u32[]{:S(2)}) %all-to-all-start.6) | async-done | bytes 1048608 | tf_op jit(solution)/shard_map/all_to_all | solution.py:34
  300.7 7.8 %all-to-all-start.1 = ((bf16[4,128,2048]{2,1,0:T(8,128)(2,1)}), bf16[4,128,2048]{2,1,0:T(8,128)(2,1)}, u32[]{:S(2)}, u32[]{:S(2)}) async-start(bf16[4,128,2048]{2,1,0:T(8,128)(2,1)} %bitcast.75), calls=%async_computation.1 | async-start | bytes 4194304 | tf_op jit(solution)/shard_map/all_to_all | solution.py:34
  308.7 1.8 fusion.47
  310.6 1.8 fusion.46
  313.0 6.2 %fusion.11 = bf16[512,2048]{1,0:T(8,128)(2,1)} fusion(bf16[1024,4096]{1,0:T(8,128)(2,1)} %all-gather.10.cloned.1.call-done, bf16[512,2048]{1,0:T(8,128)(2,1)} %bitcast.1), kind=kOutput, calls=%fused_computation.11 | convolution fusion | flops 2148532224 | bytes 7340032 | tf_op jit(solution)/shard_map/dot_general | solution.py:10
  319.2 33.8 %all-to-all-done.1 = bf16[4,128,2048]{2,1,0:T(8,128)(2,1)} async-done(((bf16[4,128,2048]{2,1,0:T(8,128)(2,1)}), bf16[4,128,2048]{2,1,0:T(8,128)(2,1)}, u32[]{:S(2)}, u32[]{:S(2)}) %all-to-all-start.1) | async-done | bytes 2097184 | tf_op jit(solution)/shard_map/all_to_all | solution.py:34
  353.0 7.8 %all-to-all-start.4 = ((bf16[4,128,2048]{2,1,0:T(8,128)(2,1)}), bf16[4,128,2048]{2,1,0:T(8,128)(2,1)}, u32[]{:S(2)}, u32[]{:S(2)}) async-start(bf16[4,128,2048]{2,1,0:T(8,128)(2,1)} %bitcast.74), calls=%async_computation.4 | async-start | bytes 4194304 | tf_op jit(solution)/shard_map/all_to_all | solution.py:34
  362.7 3.4 psum.7
  370.5 34.8 %all-to-all-done.4 = bf16[4,128,2048]{2,1,0:T(8,128)(2,1)} async-done(((bf16[4,128,2048]{2,1,0:T(8,128)(2,1)}), bf16[4,128,2048]{2,1,0:T(8,128)(2,1)}, u32[]{:S(2)}, u32[]{:S(2)}) %all-to-all-start.4) | async-done | bytes 2097184 | tf_op jit(solution)/shard_map/all_to_all | solution.py:34
  405.3 7.6 %all-to-all-start.3 = ((bf16[16,8,8192]{2,1,0:T(8,128)(2,1)}), bf16[16,8,8192]{2,1,0:T(8,128)(2,1)}, u32[]{:S(2)}, u32[]{:S(2)}) async-start(bf16[16,8,8192]{2,1,0:T(8,128)(2,1)} %maximum_bitcast_fusion), calls=%async_computation.3 | async-start | bytes 4194304 | tf_op jit(solution)/shard_map/all_to_all | solution.py:34
  425.1 2.1 convert_reduce_fusion.1
  427.2 2.1 convert_reduce_fusion
  429.3 31.6 %all-to-all-done.3 = bf16[16,8,8192]{2,1,0:T(8,128)(2,1)} async-done(((bf16[16,8,8192]{2,1,0:T(8,128)(2,1)}), bf16[16,8,8192]{2,1,0:T(8,128)(2,1)}, u32[]{:S(2)}, u32[]{:S(2)}) %all-to-all-start.3) | async-done | bytes 2097184 | tf_op jit(solution)/shard_map/all_to_all | solution.py:34
  460.9 2.2 fusion.18
  463.1 2.2 fusion.19
  465.3 2.3 fusion.20
  467.6 2.3 fusion.21
  (94 shorter events, 28.0 us)
Async XLA Ops:
  7.2 305.2 %copy-start = (bf16[16,16,2048]{2,1,0:T(8,128)(2,1)S(1)}, bf16[16,16,2048]{2,1,0:T(8,128)(2,1)}, u32[]{:S(2)}) copy-start(bf16[16,16,2048]{2,1,0:T(8,128)(2,1)} %param.20) | copy-start | bytes 3145732
  7.2 4.6 copy-start.9
  7.2 19.1 %all-gather.8.cloned.1.call-start = ((), (), s32[]{:S(2)}) async-start(), calls=%async_computation.10 | async-start | bytes 1572864 | tf_op jit(solution)/shard_map/all_gather | solution.py:137
  7.9 23.8 %all-gather.6.cloned.1.call-start = ((), (), s32[]{:S(2)}) async-start(), calls=%async_computation.9 | async-start | bytes 1572864 | tf_op jit(solution)/shard_map/all_gather | solution.py:136
  8.7 105.2 %all-gather.12.cloned.1.call-start = ((), (), s32[]{:S(2)}) async-start(), calls=%async_computation.12 | async-start | bytes 2621440 | tf_op jit(solution)/shard_map/all_gather | solution.py:144
  11.7 6.3 %copy-start.1 = (bf16[128,2048]{1,0:T(8,128)(2,1)}, bf16[128,2048]{1,0:T(8,128)(2,1)S(1)}, u32[]{:S(2)}) copy-start(bf16[128,2048]{1,0:T(8,128)(2,1)S(1)} %get-tuple-element.24) | copy-start | bytes 1572868
  11.7 3.0 copy-start.15
  11.7 185.2 %all-gather.10.cloned.1.call-start = ((), (), s32[]{:S(2)}) async-start(), calls=%async_computation.11 | async-start | bytes 10485760 | tf_op jit(solution)/shard_map/all_gather | solution.py:61
  14.7 1.0 copy-start.5
  14.7 1.3 copy-start.4
  14.7 1.7 copy-start.2
  16.7 1.4 copy-start.3
  19.1 89.6 %all-to-all-start.2 = ((bf16[16,8,8320]{2,1,0:T(8,128)(2,1)}), bf16[16,8,8320]{2,1,0:T(8,128)(2,1)S(1)}, u32[]{:S(2)}, u32[]{:S(2)}) async-start(bf16[16,8,8320]{2,1,0:T(8,128)(2,1)} %bitcast.69), calls=%async_computation.2 | async-start | bytes 4259840 | tf_op jit(solution)/shard_map/all_to_all | solution.py:34
  31.8 1.3 copy-start.10
  31.8 1.4 copy-start.11
  31.8 1.4 copy-start.12
  108.8 94.3 %all-to-all-start = ((bf16[4,128,2048]{2,1,0:T(8,128)(2,1)}), bf16[4,128,2048]{2,1,0:T(8,128)(2,1)}, u32[]{:S(2)}, u32[]{:S(2)}) async-start(bf16[4,128,2048]{2,1,0:T(8,128)(2,1)} %bitcast.68), calls=%async_computation | async-start | bytes 4194304 | tf_op jit(solution)/shard_map/all_to_all | solution.py:34
  113.3 151.3 %all-gather.14.cloned.1.call-start = ((), (), s32[]{:S(2)}) async-start(), calls=%async_computation.14 | async-start | bytes 2621440 | tf_op jit(solution)/shard_map/all_gather | solution.py:144
  203.1 67.6 %all-to-all-start.5 = ((bf16[4,128,1024]{2,1,0:T(8,128)(2,1)}), bf16[4,128,1024]{2,1,0:T(8,128)(2,1)}, u32[]{:S(2)}, u32[]{:S(2)}) async-start(bf16[4,128,1024]{2,1,0:T(8,128)(2,1)} %bitcast.82), calls=%async_computation.5 | async-start | bytes 2097152 | tf_op jit(solution)/shard_map/all_to_all | solution.py:34
  270.7 30.0 %all-to-all-start.6 = ((bf16[4,128,1024]{2,1,0:T(8,128)(2,1)}), bf16[4,128,1024]{2,1,0:T(8,128)(2,1)}, u32[]{:S(2)}, u32[]{:S(2)}) async-start(bf16[4,128,1024]{2,1,0:T(8,128)(2,1)} %bitcast.83), calls=%async_computation.7 | async-start | bytes 2097152 | tf_op jit(solution)/shard_map/all_to_all | solution.py:34
  300.7 52.3 %all-to-all-start.1 = ((bf16[4,128,2048]{2,1,0:T(8,128)(2,1)}), bf16[4,128,2048]{2,1,0:T(8,128)(2,1)}, u32[]{:S(2)}, u32[]{:S(2)}) async-start(bf16[4,128,2048]{2,1,0:T(8,128)(2,1)} %bitcast.75), calls=%async_computation.1 | async-start | bytes 4194304 | tf_op jit(solution)/shard_map/all_to_all | solution.py:34
  353.0 52.3 %all-to-all-start.4 = ((bf16[4,128,2048]{2,1,0:T(8,128)(2,1)}), bf16[4,128,2048]{2,1,0:T(8,128)(2,1)}, u32[]{:S(2)}, u32[]{:S(2)}) async-start(bf16[4,128,2048]{2,1,0:T(8,128)(2,1)} %bitcast.74), calls=%async_computation.4 | async-start | bytes 4194304 | tf_op jit(solution)/shard_map/all_to_all | solution.py:34
  366.0 1.6 copy-start.6
  366.0 2.0 copy-start.7
  366.7 1.6 copy-start.13
  367.3 1.3 copy-start.8
  405.3 55.6 %all-to-all-start.3 = ((bf16[16,8,8192]{2,1,0:T(8,128)(2,1)}), bf16[16,8,8192]{2,1,0:T(8,128)(2,1)}, u32[]{:S(2)}, u32[]{:S(2)}) async-start(bf16[16,8,8192]{2,1,0:T(8,128)(2,1)} %maximum_bitcast_fusion), calls=%async_computation.3 | async-start | bytes 4194304 | tf_op jit(solution)/shard_map/all_to_all | solution.py:34
  412.9 2.7 copy-start.14
  412.9 52.4 %reduce-scatter.3.cloned.1.call-start = ((), (), s32[]{:S(2)}) async-start(), calls=%async_computation.13 | async-start | bytes 1572864 | tf_op jit(solution)/shard_map/reduce_scatter | solution.py:156
  415.3 52.4 %reduce-scatter.5.cloned.1.call-start = ((), (), s32[]{:S(2)}) async-start(), calls=%async_computation.15 | async-start | bytes 1572864 | tf_op jit(solution)/shard_map/reduce_scatter | solution.py:156
Sparse Core Ops, SparseCore 0:
  9.5 10.3 all-gather.7
  21.5 10.2 all-gather.5
  33.9 70.9 all-gather.11
  107.2 89.6 all-gather.9
  198.9 65.5 all-gather.13
  415.6 9.5 reduce-scatter.2
  427.5 9.5 reduce-scatter.4
